TPU v7x, 32 devices: a whole 2x2x4 slice. The times are simulated.
32 devices in a mesh: seq: 8 (over z, core), expert: 4 (over y, x).
Axes of the slice: x: 2, y: 2, z: 4, core: 2. Of those that a mesh axis runs over, the one named last changes fastest.
Arguments:
- tokens: bfloat16 [4, 32, 4096], P('expert', 'seq'), may hold values from -6 to 6
- out_grad: bfloat16 [4, 32, 4096], P('expert', 'seq'), may hold values from -12 to 12
- expert_ids: int32 [4, 32, 8], P('expert', 'seq'), may hold values from 0 to 15, as said below
- route_gates: bfloat16 [4, 32, 8], P('expert', 'seq'), may hold values from 0.019897461 to 0.5
- gate_weight: bfloat16 [16, 1536, 4096], P('expert', 'seq'), may hold values from -0.09375 to 0.09375
- up_weight: bfloat16 [16, 1536, 4096], P('expert', 'seq'), may hold values from -0.09375 to 0.09375
- down_weight: bfloat16 [16, 1536, 4096], P('expert', 'seq'), may hold values from -0.15625 to 0.15625
Outputs:
- token_grad: bfloat16 [4, 32, 4096], P('expert', 'seq')
Inputs may be any that keep to these rules, and one draw needn't show every extreme that they name: `expert_ids`: each token names 8 different experts; within each index of the first dimension (one group of 32 tokens) every expert is named at most 32 times, and some expert exactly 32 times.
All inputs are finite; a program needn't handle non-finite values.
Results may differ from a plain program's by a relative error of at most 0.0057.
Values may be sent and summed in bfloat16 or wider, within the bound.
No kernel may reach another device: no remote copies, remote signals or barrier semaphores. Data moves between devices by JAX's collectives and lax.ppermute only.
A program may use at most 128 MiB of HBM per device.

v0:
```python
import jax
import jax.numpy as jnp
from jax import lax
from jax.sharding import PartitionSpec as P


def swiglu_back(gate_act, up_act, hidden_grad):
    sigmoid = jax.nn.sigmoid(gate_act)
    d_gate = (hidden_grad * up_act * sigmoid * (1.0 + gate_act * (1.0 - sigmoid))).astype(
        jnp.bfloat16
    )
    d_up = (hidden_grad * gate_act * sigmoid).astype(jnp.bfloat16)
    return (d_gate, d_up)


def expert_grads(input_rows, grad_rows, gate_rows, gate_mat, up_mat, down_mat):
    gate_act = jnp.einsum("ird,ifd->ifr", input_rows, gate_mat, preferred_element_type=jnp.float32)
    up_act = jnp.einsum("ird,ifd->ifr", input_rows, up_mat, preferred_element_type=jnp.float32)
    down_back = jnp.einsum("ird,ifd->ifr", grad_rows, down_mat, preferred_element_type=jnp.float32)
    hidden_grad = down_back * gate_rows.astype(jnp.float32)[:, None, :]
    d_gate, d_up = swiglu_back(gate_act, up_act, hidden_grad)
    summed = jnp.einsum("ifr,ifd->ird", d_gate, gate_mat, preferred_element_type=jnp.float32)
    summed = summed + jnp.einsum("ifr,ifd->ird", d_up, up_mat, preferred_element_type=jnp.float32)
    return summed.astype(jnp.bfloat16)


def per_device(tokens, out_grad, expert_ids, route_gates, gate_weight, up_weight, down_weight):
    gathered_x, gathered_dy, gathered_ids, gathered_gates = (
        lax.all_gather(tokens, "seq", axis=1, tiled=True),
        lax.all_gather(out_grad, "seq", axis=1, tiled=True),
        lax.all_gather(expert_ids, "seq", axis=1, tiled=True),
        lax.all_gather(route_gates, "seq", axis=1, tiled=True),
    )
    group_x = gathered_x[0]
    group_dy = gathered_dy[0]
    group_idx = gathered_ids[0]
    group_gates = gathered_gates[0]
    group_size, top_count = group_idx.shape
    model_width = group_x.shape[1]
    local_experts = gate_weight.shape[0]
    expert_peers = lax.axis_size("expert")
    seq_size = lax.axis_size("seq")
    experts = local_experts * expert_peers
    capacity = 2 * group_size * top_count // experts
    flat_ids = group_idx.reshape(-1)
    onehot = (flat_ids[:, None] == jnp.arange(experts, dtype=jnp.int32)[None, :]).astype(jnp.int32)
    position = jnp.sum(jnp.cumsum(onehot, axis=0) * onehot, axis=1) - 1
    slot_index = flat_ids * capacity + position
    route_token = jnp.arange(flat_ids.shape[0], dtype=jnp.int32) // top_count
    slot_token = (
        jnp.full((experts * capacity,), group_size, jnp.int32).at[slot_index].set(route_token)
    )
    slot_gate = (
        jnp.zeros((experts * capacity,), jnp.bfloat16).at[slot_index].set(group_gates.reshape(-1))
    )
    slot_owner = slot_token
    slot_token = slot_token.reshape(expert_peers, local_experts, capacity)
    slot_gate = slot_gate.reshape(expert_peers, local_experts, capacity)
    padded_x = jnp.concatenate([group_x, jnp.zeros((1, model_width), jnp.bfloat16)], axis=0)
    padded_dy = jnp.concatenate([group_dy, jnp.zeros((1, model_width), jnp.bfloat16)], axis=0)
    share_len = capacity // seq_size
    start_slot = lax.axis_index("seq") * share_len
    part_token = lax.dynamic_slice_in_dim(slot_token, start_slot, share_len, 2)
    part_gate = lax.dynamic_slice_in_dim(slot_gate, start_slot, share_len, 2)
    send_x = jnp.take(padded_x, part_token, axis=0)
    send_dy = jnp.take(padded_dy, part_token, axis=0)
    arrived_x, arrived_dy, arrived_gate = (
        lax.all_to_all(send_x, "expert", split_axis=0, concat_axis=2, tiled=True),
        lax.all_to_all(send_dy, "expert", split_axis=0, concat_axis=2, tiled=True),
        lax.all_to_all(part_gate, "expert", split_axis=0, concat_axis=2, tiled=True),
    )
    recv_x, recv_dy, recv_gate = (
        lax.all_gather(arrived_x, "seq", axis=2, tiled=True),
        lax.all_gather(arrived_dy, "seq", axis=2, tiled=True),
        lax.all_gather(arrived_gate, "seq", axis=2, tiled=True),
    )
    part_rows = expert_grads(
        recv_x[0], recv_dy[0], recv_gate[0], gate_weight, up_weight, down_weight
    )
    reshaped = part_rows.reshape(
        local_experts, seq_size, expert_peers, capacity // seq_size, model_width
    )
    returned = lax.all_to_all(reshaped, "expert", split_axis=2, concat_axis=0, tiled=True)
    flat_parts = returned.reshape(experts * capacity, model_width)
    wanted = jnp.arange(lax.axis_size("seq") * tokens.shape[1], dtype=jnp.int32)
    selector = (wanted[:, None] == slot_owner[None, :]).astype(jnp.bfloat16)
    summed = lax.psum_scatter(
        jnp.dot(selector, flat_parts, preferred_element_type=jnp.float32),
        "seq",
        scatter_dimension=0,
        tiled=True,
    )
    return summed.astype(jnp.bfloat16)[None]


def solution(mesh):
    in_specs = (
        P("expert", "seq", None),
        P("expert", "seq", None),
        P("expert", "seq", None),
        P("expert", "seq", None),
        P("expert", "seq", None),
        P("expert", "seq", None),
        P("expert", "seq", None),
    )
    out_specs = P("expert", "seq", None)
    return jax.shard_map(
        per_device, mesh=mesh, in_specs=in_specs, out_specs=out_specs, check_vma=False
    )
```

profile of v0, /device:TPU:0, one launch (start us, length us, event | category | flops | bytes accessed | tf_op | source)
XLA Modules:
  0.0 310.6 jit_solution(13137008721957007697)
XLA Ops:
  6.5 14.7 %all_gather.21 = s32[1,32,8]{2,0,1:T(1,128)S(1)} all-gather(s32[1,4,8]{2,0,1:T(1,128)} %bitcast.102), channel_id=1, replica_groups=mesh['seq'=8,'expert'=4] {'seq'}, dimensions={1}, use_global_device_ids=true | all-gather | bytes 1152 | tf_op jit(solution)/shard_map/all_gather | solution.py:31
  21.4 0.6 reduce-window.6
  22.7 0.7 fusion.50
  23.7 1.4 scatter_custom_fusion
  25.4 0.8 copy.33
  26.2 14.9 %all_gather.22 = bf16[1,32,4096]{2,0,1:T(2,128)(2,1)S(1)} all-gather(bf16[1,4,4096]{2,0,1:T(2,128)(2,1)S(1)} %copy.33), channel_id=1, replica_groups=mesh['seq'=8,'expert'=4] {'seq'}, dimensions={1}, use_global_device_ids=true | all-gather | bytes 294912 | tf_op jit(solution)/shard_map/all_gather | solution.py:30
  41.4 0.9 gather_fusion
  42.6 14.7 %all_gather.26 = bf16[1,32,4096]{2,0,1:T(2,128)(2,1)S(1)} all-gather(bf16[1,4,4096]{2,0,1:T(2,128)(2,1)S(1)} %copy.39), channel_id=1, replica_groups=mesh['seq'=8,'expert'=4] {'seq'}, dimensions={1}, use_global_device_ids=true | all-gather | bytes 294912 | tf_op jit(solution)/shard_map/all_gather | solution.py:29
  57.6 0.9 gather_fusion.1
  58.7 0.6 broadcast_select_fusion
  59.3 12.5 %all_to_all.69 = bf16[4,4,4,4096]{3,2,1,0:T(4,128)(2,1)S(1)} all-to-all(bf16[4,4,4,4096]{3,2,1,0:T(4,128)(2,1)S(1)} %get-tuple-element.10), channel_id=1, replica_groups=mesh['seq'=8,'expert'=4] {'expert'}, dimensions={0} | all-to-all | bytes 1048576 | tf_op jit(solution)/shard_map/all_to_all | solution.py:68
  72.0 0.9 all_to_all.61
  73.0 10.2 %all_to_all.70 = bf16[4,4,4,4096]{3,2,1,0:T(4,128)(2,1)S(1)} all-to-all(bf16[4,4,4,4096]{3,2,1,0:T(4,128)(2,1)S(1)} %get-tuple-element.11), channel_id=1, replica_groups=mesh['seq'=8,'expert'=4] {'expert'}, dimensions={0} | all-to-all | bytes 1048576 | tf_op jit(solution)/shard_map/all_to_all | solution.py:69
  83.4 0.9 all_to_all.53
  84.4 13.4 %all_gather.24 = bf16[1,32,8]{2,0,1:T(2,128)(2,1)S(1)} all-gather(bf16[1,4,8]{2,0,1:T(2,128)(2,1)S(1)} %copy.35), channel_id=1, replica_groups=mesh['seq'=8,'expert'=4] {'seq'}, dimensions={1}, use_global_device_ids=true | all-gather | bytes 576 | tf_op jit(solution)/shard_map/all_gather | solution.py:32
  98.0 2.2 scatter_custom_fusion.1
  100.3 7.0 %all_to_all.71 = bf16[4,4,4]{2,1,0:T(4,128)(2,1)S(1)} all-to-all(bf16[4,4,4]{2,1,0:T(4,128)(2,1)S(1)} %constant_dynamic-slice_fusion), channel_id=1, replica_groups=mesh['seq'=8,'expert'=4] {'expert'}, dimensions={0} | all-to-all | bytes 256 | tf_op jit(solution)/shard_map/all_to_all | solution.py:70
  107.5 14.3 %all_gather.25 = bf16[1,4,128]{1,0,2:T(2,128)(2,1)S(1)} all-gather(bf16[1,4,16]{1,0,2:T(2,128)(2,1)S(1)} %reshape.126), channel_id=1, replica_groups=mesh['seq'=8,'expert'=4] {'seq'}, dimensions={2}, use_global_device_ids=true | all-gather | bytes 1152 | tf_op jit(solution)/shard_map/all_gather | solution.py:75
  121.9 5.9 %fusion.9 = f32[4,192,128]{2,1,0:T(8,128)S(1)} fusion(bf16[4,192,4096]{2,1,0:T(8,128)(2,1)} %param.13, bf16[1,4,128,4096]{3,2,1,0:T(8,128)(2,1)} %all-gather.5.cloned.1.call-done), kind=kOutput, calls=%fused_computation.12 | convolution fusion | flops 805306368 | bytes 10878976 | tf_op jit(solution)/shard_map/ird,ifd->ifr/dot_general | solution.py:17
  127.9 38.2 %all-gather.3.cloned.1.call-done = bf16[1,4,128,4096]{3,2,1,0:T(8,128)(2,1)} async-done(((bf16[1,4,16,4096]{3,2,1,0:T(8,128)(2,1)}), bf16[1,4,128,4096]{3,2,1,0:T(8,128)(2,1)}) %all-gather.3.cloned.1.call-update) | async-done | bytes 4194320 | tf_op jit(solution)/shard_map/all_gather | solution.py:74
  166.1 5.8 %fusion.24 = f32[4,192,128]{2,1,0:T(8,128)S(1)} fusion(bf16[4,192,4096]{2,1,0:T(8,128)(2,1)} %param.15, bf16[1,4,128,4096]{3,2,1,0:T(8,128)(2,1)} %all-gather.3.cloned.1.call-done, f32[4,128]{1,0:T(4,128)S(1)} %copy.38), kind=kOutput, calls=%fused_computation.17 | convolution fusion | flops 805404672 | bytes 10881024 | tf_op jit(solution)/shard_map/ird,ifd->ifr/dot_general | solution.py:19
  171.9 11.9 %fusion.31 = f32[4,128,4096]{2,1,0:T(8,128)} fusion(bf16[4,192,4096]{2,1,0:T(8,128)(2,1)} %param.13, f32[4,192,128]{2,1,0:T(8,128)S(1)} %fusion.24, bf16[4,192,4096]{2,1,0:T(8,128)(2,1)} %param.14, bf16[1,4,128,4096]{3,2,1,0:T(8,128)(2,1)} %all-gather.5.cloned.1.call-done, f32[4,192,128]{2,1,0:T(8,128)S(1)} %fusion.9), kind=kOutput, calls=%fused_computation.19 | convolution fusion | flops 1611595776 | bytes 25952256 | tf_op jit(solution)/shard_map/ifr,ifd->ird/dot_general | solution.py:22
  183.8 8.5 %add_convert_fusion = bf16[4,128,4096]{2,1,0:T(8,128)(2,1)} fusion(f32[4,128,4096]{2,1,0:T(8,128)} %fusion.31, bf16[4,192,4096]{2,1,0:T(8,128)(2,1)} %param.14, f32[4,192,128]{2,1,0:T(8,128)S(1)} %fusion.24, f32[4,192,128]{2,1,0:T(8,128)S(1)} %fusion.9), kind=kOutput, calls=%fused_computation.4 | convolution fusion | flops 810090496 | bytes 19660800 | tf_op jit(solution)/shard_map/ifr,ifd->ird/dot_general | solution.py:23
  192.4 7.2 %reshape.79 = bf16[4,8,4,4,4096]{4,3,2,1,0:T(4,128)(2,1)} reshape(bf16[4,128,4096]{2,1,0:T(8,128)(2,1)} %add_convert_fusion) | data formatting | bytes 8388608 | tf_op jit(solution)/shard_map/reshape | solution.py:80
  199.6 7.9 %copy.41 = bf16[4,8,4,4,4096]{4,3,1,0,2:T(4,128)(2,1)} copy(bf16[4,8,4,4,4096]{4,3,2,1,0:T(4,128)(2,1)} %reshape.79) | data formatting | bytes 8388608 | tf_op jit(solution)/shard_map/reshape | solution.py:80
  207.4 5.0 %all-to-all-start.3 = ((bf16[4,8,4,4,4096]{4,3,1,0,2:T(4,128)(2,1)}), bf16[4,8,4,4,4096]{4,3,1,0,2:T(4,128)(2,1)}, u32[]{:S(2)}, u32[]{:S(2)}) async-start(bf16[4,8,4,4,4096]{4,3,1,0,2:T(4,128)(2,1)} %copy.41), calls=%async_computation.3 | async-start | bytes 8388608 | tf_op jit(solution)/shard_map/all_to_all | solution.py:83
  212.5 0.6 dynamic-slice
  213.7 46.8 %all-to-all-done.3 = bf16[4,8,4,4,4096]{4,3,1,0,2:T(4,128)(2,1)} async-done(((bf16[4,8,4,4,4096]{4,3,1,0,2:T(4,128)(2,1)}), bf16[4,8,4,4,4096]{4,3,1,0,2:T(4,128)(2,1)}, u32[]{:S(2)}, u32[]{:S(2)}) %all-to-all-start.3) | async-done | bytes 4194336 | tf_op jit(solution)/shard_map/all_to_all | solution.py:83
  260.5 6.9 %reshape.80 = bf16[512,4096]{1,0:T(8,128)(2,1)} reshape(bf16[4,4,8,1,4,4096]{5,4,2,1,0,3:T(4,128)(2,1)} %bitcast.17) | data formatting | bytes 8388608 | tf_op jit(solution)/shard_map/reshape | solution.py:84
  267.4 3.0 fusion.38
  270.4 32.7 %all-reduce.4 = bf16[32,4096]{1,0:T(8,128)(2,1)S(1)} all-reduce(f32[32,4096]{1,0:T(8,128)S(1)} %fusion.38), channel_id=2, replica_groups=mesh['seq'=8,'expert'=4] {'seq'}, use_global_device_ids=true, to_apply=%region_5.7.clone | all-reduce | flops 131072 | bytes 786432
  303.1 0.6 fusion.39
  (45 shorter events, 3.5 us)
Async XLA Ops:
  6.5 36.0 %copy-start = (bf16[1,4,4096]{2,1,0:T(4,128)(2,1)S(1)}, bf16[1,4,4096]{2,1,0:T(4,128)(2,1)}, u32[]{:S(2)}) copy-start(bf16[1,4,4096]{2,1,0:T(4,128)(2,1)} %param.9) | copy-start | bytes 98308
  6.5 115.4 %all-gather.5.cloned.1.call-start = ((), (), s32[]{:S(2)}) async-start(), calls=%async_computation.5 | async-start | bytes 4718592 | tf_op jit(solution)/shard_map/all_gather | solution.py:73
  58.5 25.9 %copy-start.1 = (bf16[1,4,8]{2,1,0:T(4,128)(2,1)S(1)}, bf16[1,4,8]{2,1,0:T(4,128)(2,1)}, u32[]{:S(2)}) copy-start(bf16[1,4,8]{2,1,0:T(4,128)(2,1)} %param.12) | copy-start | bytes 196
  72.9 93.1 %all-gather.3.cloned.1.call-start = ((), (), s32[]{:S(2)}) async-start(), calls=%async_computation.4 | async-start | bytes 4718592 | tf_op jit(solution)/shard_map/all_gather | solution.py:74
  207.4 5.0 %copy-start.2 = (u32[32]{0:T(128)S(1)}, u32[32]{0:T(128)}, u32[]{:S(2)}) copy-start(u32[32]{0:T(128)} %constant.65) | copy-start | bytes 388
  207.4 53.1 %all-to-all-start.3 = ((bf16[4,8,4,4,4096]{4,3,1,0,2:T(4,128)(2,1)}), bf16[4,8,4,4,4096]{4,3,1,0,2:T(4,128)(2,1)}, u32[]{:S(2)}, u32[]{:S(2)}) async-start(bf16[4,8,4,4,4096]{4,3,1,0,2:T(4,128)(2,1)} %copy.41), calls=%async_computation.3 | async-start | bytes 8388608 | tf_op jit(solution)/shard_map/all_to_all | solution.py:83
Sparse Core Ops, SparseCore 0:
  73.1 45.5 all-gather.4
  120.3 45.7 all-gather.2
where the time goes:
time: 311 us
  blocking collectives  134 us (43%)
  waiting for transfers between devices  85.1 us (27%)
  matrix products  35.2 us (11%)
  local copies, waits for them, and re-layouts  34.3 us (11%)
  between operations  14.3 us (5%)
  starting transfers between devices  5.03 us (2%)
    all_to_all x1, waiting for transfers between devices, per_device(): lax.all_to_all(reshaped, 'expert', split_axis=2, concat_axis=0, tiled=True)  46.8 us
    all_gather x1, waiting for transfers between devices, per_device(): lax.all_gather(arrived_dy, 'seq', axis=2, tiled=True)  38.2 us
    unnamed x1, blocking collectives  32.7 us
    reshape x2, local copies, waits for them, and re-layouts, per_device(): part_rows.reshape(local_experts, seq_size, expert_peers, capacity // seq_...  15.1 us
    all_gather x1, blocking collectives, per_device(): lax.all_gather(out_grad, 'seq', axis=1, tiled=True)  14.9 us
    all_gather x1, blocking collectives, per_device(): lax.all_gather(expert_ids, 'seq', axis=1, tiled=True)  14.7 us
    all_gather x1, blocking collectives, per_device(): lax.all_gather(tokens, 'seq', axis=1, tiled=True)  14.7 us
    all_gather x1, blocking collectives, per_device(): lax.all_gather(arrived_gate, 'seq', axis=2, tiled=True)  14.3 us
  transfers between devices with their start and end apart: 3, of which 2 were waited for; matrix products, arithmetic and copies ran while one was open for 3% of the time, Pallas kernels for 0%

commit v1 on v0

v1 whole, which is shorter than its diff:
```python
import jax
import jax.numpy as jnp
from jax import lax
from jax.sharding import Mesh, PartitionSpec as P

LANES = 128


def physical_mesh(mesh):
    devices = mesh.devices
    cores = len({d.core_on_chip for d in devices.flat})
    size_x = len({d.coords[0] for d in devices.flat})
    seq, expert = devices.shape
    shape = (seq // cores, cores, expert // size_x, size_x)
    return Mesh(devices.reshape(shape), ("z", "c", "y", "x"))


def swap_pairs(sizes, flip):
    cores, size_y, size_x = sizes
    flat = lambda c, y, x: (c * size_y + y) * size_x + x
    return [
        (flat(c, y, x), flat(*flip(c, y, x)))
        for c in range(cores)
        for y in range(size_y)
        for x in range(size_x)
    ]


def dense_gates(ids, gates, width):
    lane = lax.broadcasted_iota(jnp.int32, (1, 1, width), 2)
    hit = ids[:, :, None] == lane
    return jnp.sum(jnp.where(hit, gates[:, :, None].astype(jnp.float32), 0.0), axis=1).astype(jnp.bfloat16)


def per_device(sizes, tokens, out_grad, expert_ids, route_gates, gate_weight, up_weight, down_weight):
    size_z, cores, size_y, size_x = sizes
    x, dy, ids, gates = tokens[0], out_grad[0], expert_ids[0], route_gates[0]
    count, width = x.shape
    local, hidden, _ = gate_weight.shape
    experts = local * size_y * size_x
    pad = -(-experts // LANES) * LANES
    core = lax.axis_index("c")
    first = core == 0
    trio = ("c", "y", "x")
    swap = [(0, 1), (1, 0)]
    near = [
        swap_pairs((cores, size_y, size_x), lambda c, y, x, k=k: (c, y, x ^ k) if c == 0 else (c, y ^ k, x))
        for k in range(1, size_x)
    ]
    far = [
        swap_pairs((cores, size_y, size_x), lambda c, y, x, k=k: (c, y ^ k, x) if c == 0 else (c, y, x ^ k))
        for k in range(1, size_x)
    ]
    column = [[(z, z ^ k) for z in range(size_z)] for k in range(1, size_z)]

    dense = dense_gates(ids, gates, pad)
    xg = jnp.concatenate([x, dense], axis=1)
    dg = jnp.concatenate([dy, jnp.zeros_like(dense)], axis=1)
    keep, send = jnp.where(first, xg, dg), jnp.where(first, dg, xg)
    got = lax.ppermute(send, "c", swap)
    block = jnp.concatenate([jnp.where(first, keep, got), jnp.where(first, got, keep)], axis=0)
    block = jnp.concatenate([block] + [lax.ppermute(block, "z", p) for p in column], axis=0)
    block = jnp.concatenate([block] + [lax.ppermute(block, trio, p) for p in near], axis=0)
    block = jnp.concatenate([block] + [lax.ppermute(block, trio, p) for p in far], axis=0)
    other = lax.ppermute(block, "c", swap)
    rows = block.shape[0]
    unit = rows // (size_x * size_y)
    turn = lambda a: a.reshape(size_x, size_x, -1, a.shape[-1]).swapaxes(0, 1).reshape(a.shape)
    other = turn(other)
    all_x = jnp.where(first, block, other)
    all_dy = jnp.where(first, other, block)[:, :width]
    all_gates = all_x[:, width:]
    all_x = all_x[:, :width]

    me = lax.axis_index(("y", "x"))
    gate_mat, up_mat, down_mat = (
        w.reshape(local * hidden, width) for w in (gate_weight, up_weight, down_weight)
    )
    owner = me * local + lax.broadcasted_iota(jnp.int32, (pad, local * hidden), 1) // hidden
    spread = (lax.broadcasted_iota(jnp.int32, (pad, local * hidden), 0) == owner).astype(jnp.bfloat16)
    dot_t = lambda a, w: lax.dot_general(a, w, (((1,), (1,)), ((), ())), preferred_element_type=jnp.float32)
    gate_act = dot_t(all_x, gate_mat)
    up_act = dot_t(all_x, up_mat)
    down_back = dot_t(all_dy, down_mat)
    weight = jnp.dot(all_gates, spread, preferred_element_type=jnp.float32)
    hidden_grad = down_back * weight
    sigmoid = jax.nn.sigmoid(gate_act)
    d_gate = (hidden_grad * up_act * sigmoid * (1.0 + gate_act * (1.0 - sigmoid))).astype(jnp.bfloat16)
    d_up = (hidden_grad * gate_act * sigmoid).astype(jnp.bfloat16)
    pick = lambda d: d.reshape(-1, cores, count, d.shape[-1]).swapaxes(0, 1).reshape(d.shape)
    d_gate, d_up = pick(d_gate), pick(d_up)
    part = jnp.dot(d_gate, gate_mat, preferred_element_type=jnp.float32)
    part = part + jnp.dot(d_up, up_mat, preferred_element_type=jnp.float32)
    half = rows // cores
    mine = jnp.where(first, part[:half], part[half:])
    away = jnp.where(first, part[half:], part[:half]).astype(jnp.bfloat16)
    mine = mine + turn(lax.ppermute(away, "c", swap)).astype(jnp.float32)

    def reduce_over(mine, axes, moves):
        n = len(moves) + 1
        parts = mine.reshape(n, -1, mine.shape[-1])
        total = parts[0]
        for k, pairs in enumerate(moves, 1):
            total = total + lax.ppermute(parts[k].astype(jnp.bfloat16), axes, pairs).astype(jnp.float32)
        return total

    mine = reduce_over(mine, trio, far)
    mine = reduce_over(mine, trio, near)
    mine = reduce_over(mine, "z", column)
    return mine.astype(jnp.bfloat16)[None]


def solution(mesh):
    phys = physical_mesh(mesh)
    sizes = tuple(phys.shape[n] for n in ("z", "c", "y", "x"))
    spec = P(("y", "x"), ("z", "c"), None)

    def step(*args):
        return per_device(sizes, *args)

    return jax.shard_map(step, mesh=phys, in_specs=(spec,) * 7, out_specs=spec, check_vma=False)
```

time: 311 us -> 76.8 us (0.25)
  blocking collectives: 134 us -> 0 us
  waiting for transfers between devices: 85.1 us -> 35.9 us
  local copies, waits for them, and re-layouts: 34.3 us -> 1.96 us
  matrix products: 35.2 us -> 17.7 us
  between operations: 14.3 us -> 0.27 us
  starting transfers between devices: 5.03 us -> 16.3 us
    all_gather x5 -> x0, blocking collectives: 72.1 us -> none  [the longest x1 14.9 us: per_device(): lax.all_gather(out_grad, 'seq', axis=1, tiled=True)]
    all_to_all x1 -> x0, waiting for transfers between devices: 46.8 us -> none  [per_device(): lax.all_to_all(reshaped, 'expert', split_axis=2, concat_axis=0, tiled=True)]
    all_gather x2 -> x0, waiting for transfers between devices: 38.2 us -> none  [the longest x1 38.2 us: per_device(): lax.all_gather(arrived_dy, 'seq', axis=2, tiled=True)]
    ppermute x0 -> x13, waiting for transfers between devices: none -> 35.9 us  [the longest x2 12.8 us: per_device(): lax.ppermute(block, trio, p)]
    unnamed x1 -> x0, blocking collectives: 32.7 us -> none
    all_to_all x3 -> x0, blocking collectives: 29.8 us -> none  [the longest x1 12.5 us: per_device(): lax.all_to_all(send_x, 'expert', split_axis=0, concat_axis=2, tiled=True)]
    reshape x5 -> x7, local copies, waits for them, and re-layouts: 22.1 us -> 0.42 us  [the longest x6 0.35 us: per_device(): d.reshape(-1, cores, count, d.shape[-1]).swapaxes(0, 1).reshape(d.shape)]
    dot_general x5 -> x6, matrix products: 35.2 us -> 17.7 us  [the longest x3 12.4 us: per_device(): lax.dot_general(a, w, (((1,), (1,)), ((), ())), preferred_element_type=jn...]
  transfers between devices with their start and end apart: 3 -> 13, of which waited for: 2 -> 12; matrix products, arithmetic and copies ran while one was open for 3% -> 0% of each run, Pallas kernels for 0% -> 0%
where the time goes in v1:
time: 76.8 us; the launch traced here: 76.5 us
  waiting for transfers between devices  35.9 us (47%)
  matrix products  17.7 us (23%)
  starting transfers between devices  16.3 us (21%)
  other arithmetic  4.4 us (6%)
  local copies, waits for them, and re-layouts  1.96 us (3%)
    ppermute x2, waiting for transfers between devices, per_device(): lax.ppermute(block, trio, p)  12.8 us
    ppermute x5, waiting for transfers between devices, reduce_over(): lax.ppermute(parts[k].astype(jnp.bfloat16), axes, pairs).astype(jnp.float32)  12.4 us
    dot_general x3, matrix products, per_device(): lax.dot_general(a, w, (((1,), (1,)), ((), ())), preferred_element_type=jn...  12.4 us
    ppermute x5, starting transfers between devices, reduce_over(): lax.ppermute(parts[k].astype(jnp.bfloat16), axes, pairs).astype(jnp.float32)  6.69 us
    ppermute x3, starting transfers between devices, per_device(): lax.ppermute(block, 'z', p)  5.64 us
    ppermute x3, waiting for transfers between devices, per_device(): lax.ppermute(block, 'z', p)  5.4 us
    dot_general x1, matrix products, per_device(): part = jnp.dot(d_gate, gate_mat, preferred_element_type=jnp.float32)  3.93 us
    ppermute x2, starting transfers between devices, per_device(): lax.ppermute(block, trio, p)  3.13 us
  transfers between devices with their start and end apart: 13, of which 12 were waited for; matrix products, arithmetic and copies ran while one was open for 0% of the time, Pallas kernels for 0%

profile of v1, /device:TPU:0, one launch (start us, length us, event | category | flops | bytes accessed | tf_op | source)
XLA Modules:
  0.0 76.5 jit_solution(822323011472923240)
XLA Ops:
  0.0 0.7 bitcast_convert_fusion
  0.7 0.8 %select_reduce_fusion = bf16[4,128]{1,0:T(4,128)(2,1)S(1)} fusion(f32[4,8]{1,0:T(4,128)S(1)} %bitcast_convert_fusion, s32[4,8]{1,0:T(4,128)} %bitcast.50), kind=kLoop, calls=%fused_computation.42 | loop fusion | flops 11776 | bytes 1280 | tf_op jit(solution)/shard_map/reduce_sum | solution.py:32
  1.4 0.8 %broadcast_select_fusion.3 = bf16[4,4224]{1,0:T(4,128)(2,1)S(1)} fusion(pred[]{:T(512)S(6)} %eq.21, bf16[4,4096]{1,0:T(4,128)(2,1)} %bitcast.46, bf16[4,128]{1,0:T(4,128)(2,1)S(1)} %select_reduce_fusion, bf16[4,4096]{1,0:T(4,128)(2,1)} %bitcast.48), kind=kLoop, calls=%fused_computation.38 | loop fusion | flops 84480 | bytes 100353 | tf_op jit(solution)/shard_map/jit(_where)/select_n | solution.py:59
  2.8 0.9 %collective-permute-done = bf16[4,4224]{1,0:T(4,128)(2,1)S(1)} collective-permute-done((bf16[4,4224]{1,0:T(4,128)(2,1)S(1)}, bf16[4,4224]{1,0:T(4,128)(2,1)S(1)}, u32[]{:S(2)}, u32[]{:S(2)}) %collective-permute-start) | collective-permute-done | bytes 33824 | tf_op jit(solution)/shard_map/ppermute | solution.py:60
  3.7 0.8 %broadcast_select_fusion.1 = (bf16[4,4224]{1,0:T(4,128)(2,1)S(1)}, bf16[4,4224]{1,0:T(4,128)(2,1)S(1)}) fusion(bf16[4,4224]{1,0:T(4,128)(2,1)S(1)} %collective-permute-done, pred[]{:T(512)S(6)} %eq.21, bf16[4,4096]{1,0:T(4,128)(2,1)} %bitcast.47, bf16[4,128]{1,0:T(4,128)(2,1)S(1)} %select_reduce_fusion, bf16[4,4096]{1,0:T(4,128)(2,1)} %bitcast.49), kind=kLoop, calls=%fused_computation.36 | loop fusion | flops 118272 | bytes 167937 | tf_op jit(solution)/shard_map/jit(_where)/select_n | solution.py:61
  4.6 5.0 %collective-permute-start.3 = (bf16[8,4224]{1,0:T(8,128)(2,1)S(1)}, bf16[8,4224]{1,0:T(8,128)(2,1)S(1)}, u32[]{:S(2)}, u32[]{:S(2)}) collective-permute-start(bf16[8,4224]{1,0:T(8,128)(2,1)S(1)} %pad_maximum_fusion), channel_id=1, source_target_pairs={{0,24},{8,16},{16,8},{24,0},{1,25},{9,17},{17,9},{25,1},{2,26},{10... | collective-permute-start | bytes 202760 | tf_op jit(solution)/shard_map/ppermute | solution.py:62
  9.6 0.6 collective-permute-start.1
  10.2 2.1 %collective-permute-done.3 = bf16[8,4224]{1,0:T(8,128)(2,1)S(1)} collective-permute-done((bf16[8,4224]{1,0:T(8,128)(2,1)S(1)}, bf16[8,4224]{1,0:T(8,128)(2,1)S(1)}, u32[]{:S(2)}, u32[]{:S(2)}) %collective-permute-start.3) | collective-permute-done | bytes 67616 | tf_op jit(solution)/shard_map/ppermute | solution.py:62
  12.3 3.3 %collective-permute-done.2 = bf16[8,4224]{1,0:T(8,128)(2,1)S(1)} collective-permute-done((bf16[8,4224]{1,0:T(8,128)(2,1)S(1)}, bf16[8,4224]{1,0:T(8,128)(2,1)S(1)}, u32[]{:S(2)}, u32[]{:S(2)}) %collective-permute-start.2) | collective-permute-done | bytes 67616 | tf_op jit(solution)/shard_map/ppermute | solution.py:62
  15.7 1.5 %collective-permute-start.4 = (bf16[32,4224]{1,0:T(8,128)(2,1)S(1)}, bf16[32,4224]{1,0:T(8,128)(2,1)S(1)}, u32[]{:S(2)}, u32[]{:S(2)}) collective-permute-start(bf16[32,4224]{1,0:T(8,128)(2,1)S(1)} %concatenate.24), channel_id=1, source_target_pairs={{0,1},{1,0},{2,3},{3,2},{4,6},{5,7},{6,4},{7,5},{8,9},{9,8},{10,11... | collective-permute-start | bytes 811016 | tf_op jit(solution)/shard_map/ppermute | solution.py:63
  17.3 5.0 %collective-permute-done.4 = bf16[32,4224]{1,0:T(8,128)(2,1)S(1)} collective-permute-done((bf16[32,4224]{1,0:T(8,128)(2,1)S(1)}, bf16[32,4224]{1,0:T(8,128)(2,1)S(1)}, u32[]{:S(2)}, u32[]{:S(2)}) %collective-permute-start.4) | collective-permute-done | bytes 270368 | tf_op jit(solution)/shard_map/ppermute | solution.py:63
  22.5 1.6 %collective-permute-start.5 = (bf16[64,4224]{1,0:T(8,128)(2,1)S(1)}, bf16[64,4224]{1,0:T(8,128)(2,1)S(1)}, u32[]{:S(2)}, u32[]{:S(2)}) collective-permute-start(bf16[64,4224]{1,0:T(8,128)(2,1)S(1)} %concatenate.25), channel_id=1, source_target_pairs={{0,2},{1,3},{2,0},{3,1},{4,5},{5,4},{6,7},{7,6},{8,10},{9,11},{10,... | collective-permute-start | bytes 1622024 | tf_op jit(solution)/shard_map/ppermute | solution.py:64
  24.0 7.8 %collective-permute-done.5 = bf16[64,4224]{1,0:T(8,128)(2,1)S(1)} collective-permute-done((bf16[64,4224]{1,0:T(8,128)(2,1)S(1)}, bf16[64,4224]{1,0:T(8,128)(2,1)S(1)}, u32[]{:S(2)}, u32[]{:S(2)}) %collective-permute-start.5) | collective-permute-done | bytes 540704 | tf_op jit(solution)/shard_map/ppermute | solution.py:64
  32.4 2.7 %collective-permute-done.6 = bf16[128,4224]{1,0:T(8,128)(2,1)S(1)} collective-permute-done((bf16[128,4224]{1,0:T(8,128)(2,1)S(1)}, bf16[128,4224]{1,0:T(8,128)(2,1)S(1)}, u32[]{:S(2)}, u32[]{:S(2)}) %collective-permute-start.6) | collective-permute-done | bytes 1081376 | tf_op jit(solution)/shard_map/ppermute | solution.py:65
  35.4 5.1 %fusion.5 = f32[128,768]{1,0:T(8,128)S(1)} fusion(bf16[768,4096]{1,0:T(8,128)(2,1)} %bitcast.35, bf16[128,4224]{1,0:T(8,128)(2,1)S(1)} %broadcast_select_fusion), kind=kOutput, calls=%fused_computation.13 | convolution fusion | flops 805306368 | bytes 7733248 | tf_op jit(solution)/shard_map/dot_general | solution.py:81
  40.8 2.3 %multiply_convert_fusion = (bf16[128,768]{1,0:T(8,128)(2,1)S(1)}, f32[128,768]{1,0:T(8,128)S(1)}) fusion(f32[128,768]{1,0:T(8,128)S(1)} %fusion.5, f32[128,768]{1,0:T(8,128)S(1)} %fusion.8, bf16[768,4096]{1,0:T(8,128)(2,1)S(1)} %bitcast.53, bf16[128,4224]{1,0:T(8,128)(2,1)S(1)} %concatenate.26, bf16[128,4224]{1,0:T(8,128)(2,1)S(1)} %bitcast.41, pred[]{:T(512)S(6)} %eq.21), kind=kOutput, calls=%fused_computation.18 | convolution fusion | flops 806518784 | bytes 9764865 | tf_op jit(solution)/shard_map/dot_general | solution.py:81
  43.3 5.0 %fusion.2 = bf16[128,768]{1,0:T(8,128)(2,1)S(1)} fusion(f32[128,768]{1,0:T(8,128)S(1)} %get-tuple-element.13, bf16[768,4096]{1,0:T(8,128)(2,1)} %bitcast.37, bf16[128,4224]{1,0:T(8,128)(2,1)S(1)} %broadcast_select_fusion, f32[128,768]{1,0:T(8,128)S(1)} %fusion.5), kind=kOutput, calls=%fused_computation.5 | convolution fusion | flops 806289408 | bytes 8323072 | tf_op jit(solution)/shard_map/dot_general | solution.py:81
  48.5 3.9 %fusion.23 = f32[128,4096]{1,0:T(8,128)S(1)} fusion(bf16[128,768]{1,0:T(8,128)(2,1)S(1)} %reshape.68, bf16[768,4096]{1,0:T(8,128)(2,1)} %bitcast.36), kind=kOutput, calls=%fused_computation.54 | convolution fusion | flops 805306368 | bytes 8585216 | tf_op jit(solution)/shard_map/dot_general | solution.py:92
  52.4 0.6 slice-done.1
  53.0 1.1 %convolution_add_fusion = f32[128,4096]{1,0:T(8,128)S(1)} fusion(f32[128,4096]{1,0:T(8,128)S(1)} %fusion.23, bf16[128,768]{1,0:T(8,128)(2,1)S(1)} %reshape.70, bf16[768,4096]{1,0:T(8,128)(2,1)S(1)} %bitcast.40), kind=kOutput, calls=%fused_computation | convolution fusion | flops 805830656 | bytes 10682368 | tf_op jit(solution)/shard_map/dot_general | solution.py:93
  54.4 1.8 %collective-permute-done.7 = bf16[64,4096]{1,0:T(8,128)(2,1)S(1)} collective-permute-done((bf16[64,4096]{1,0:T(8,128)(2,1)S(1)}, bf16[64,4096]{1,0:T(8,128)(2,1)S(1)}, u32[]{:S(2)}, u32[]{:S(2)}) %collective-permute-start.7) | collective-permute-done | bytes 524320 | tf_op jit(solution)/shard_map/ppermute | solution.py:97
  56.6 1.6 %collective-permute-start.8 = (bf16[32,4096]{1,0:T(8,128)(2,1)S(1)}, bf16[32,4096]{1,0:T(8,128)(2,1)S(1)}, u32[]{:S(2)}, u32[]{:S(2)}) collective-permute-start(bf16[32,4096]{1,0:T(8,128)(2,1)S(1)} %slice.110), channel_id=1, source_target_pairs={{0,2},{1,3},{2,0},{3,1},{4,5},{5,4},{6,7},{7,6},{8,10},{9,11},{10,... | collective-permute-start | bytes 786440 | tf_op jit(solution)/shard_map/ppermute | solution.py:104
  58.2 4.9 %collective-permute-done.8 = bf16[32,4096]{1,0:T(8,128)(2,1)S(1)} collective-permute-done((bf16[32,4096]{1,0:T(8,128)(2,1)S(1)}, bf16[32,4096]{1,0:T(8,128)(2,1)S(1)}, u32[]{:S(2)}, u32[]{:S(2)}) %collective-permute-start.8) | collective-permute-done | bytes 262176 | tf_op jit(solution)/shard_map/ppermute | solution.py:104
  63.1 1.6 %collective-permute-start.9 = (bf16[16,4096]{1,0:T(8,128)(2,1)S(1)}, bf16[16,4096]{1,0:T(8,128)(2,1)S(1)}, u32[]{:S(2)}, u32[]{:S(2)}) collective-permute-start(bf16[16,4096]{1,0:T(8,128)(2,1)S(1)} %slice.111), channel_id=1, source_target_pairs={{0,1},{1,0},{2,3},{3,2},{4,6},{5,7},{6,4},{7,5},{8,9},{9,8},{10,11... | collective-permute-start | bytes 393224 | tf_op jit(solution)/shard_map/ppermute | solution.py:104
  64.7 3.5 %collective-permute-done.9 = bf16[16,4096]{1,0:T(8,128)(2,1)S(1)} collective-permute-done((bf16[16,4096]{1,0:T(8,128)(2,1)S(1)}, bf16[16,4096]{1,0:T(8,128)(2,1)S(1)}, u32[]{:S(2)}, u32[]{:S(2)}) %collective-permute-start.9) | collective-permute-done | bytes 131104 | tf_op jit(solution)/shard_map/ppermute | solution.py:104
  68.2 1.2 %collective-permute-start.10 = (bf16[4,4096]{1,0:T(4,128)(2,1)S(1)}, bf16[4,4096]{1,0:T(4,128)(2,1)S(1)}, u32[]{:S(2)}, u32[]{:S(2)}) collective-permute-start(bf16[4,4096]{1,0:T(4,128)(2,1)S(1)} %get-tuple-element.7), channel_id=1, source_target_pairs={{0,8},{8,0},{16,24},{24,16},{1,9},{9,1},{17,25},{25,17},{2,10},{10... | collective-permute-start | bytes 98312 | tf_op jit(solution)/shard_map/ppermute | solution.py:104
  69.4 1.6 %collective-permute-start.12 = (bf16[4,4096]{1,0:T(4,128)(2,1)S(1)}, bf16[4,4096]{1,0:T(4,128)(2,1)S(1)}, u32[]{:S(2)}, u32[]{:S(2)}) collective-permute-start(bf16[4,4096]{1,0:T(4,128)(2,1)S(1)} %get-tuple-element.8), channel_id=1, source_target_pairs={{0,24},{8,16},{16,8},{24,0},{1,25},{9,17},{17,9},{25,1},{2,26},{10... | collective-permute-start | bytes 98312 | tf_op jit(solution)/shard_map/ppermute | solution.py:104
  71.0 0.7 collective-permute-start.11
  71.8 0.9 %collective-permute-done.10 = bf16[4,4096]{1,0:T(4,128)(2,1)S(1)} collective-permute-done((bf16[4,4096]{1,0:T(4,128)(2,1)S(1)}, bf16[4,4096]{1,0:T(4,128)(2,1)S(1)}, u32[]{:S(2)}, u32[]{:S(2)}) %collective-permute-start.10) | collective-permute-done | bytes 32800 | tf_op jit(solution)/shard_map/ppermute | solution.py:104
  72.6 2.5 %collective-permute-done.12 = bf16[4,4096]{1,0:T(4,128)(2,1)S(1)} collective-permute-done((bf16[4,4096]{1,0:T(4,128)(2,1)S(1)}, bf16[4,4096]{1,0:T(4,128)(2,1)S(1)}, u32[]{:S(2)}, u32[]{:S(2)}) %collective-permute-start.12) | collective-permute-done | bytes 32800 | tf_op jit(solution)/shard_map/ppermute | solution.py:104
  75.1 0.8 collective-permute-done.11
  75.9 0.6 fusion.16
  (38 shorter events, 3.1 us)
Async XLA Ops:
  2.3 1.4 %collective-permute-start = (bf16[4,4224]{1,0:T(4,128)(2,1)S(1)}, bf16[4,4224]{1,0:T(4,128)(2,1)S(1)}, u32[]{:S(2)}, u32[]{:S(2)}) collective-permute-start(bf16[4,4224]{1,0:T(4,128)(2,1)S(1)} %broadcast_select_fusion.3), channel_id=1, source_target_pairs={{0,4},{4,0},{1,5},{5,1},{2,6},{6,2},{3,7},{7,3},{8,12},{12,8},{9,1... | collective-permute-start | bytes 101384 | tf_op jit(solution)/shard_map/ppermute | solution.py:60
  4.6 7.7 %collective-permute-start.3 = (bf16[8,4224]{1,0:T(8,128)(2,1)S(1)}, bf16[8,4224]{1,0:T(8,128)(2,1)S(1)}, u32[]{:S(2)}, u32[]{:S(2)}) collective-permute-start(bf16[8,4224]{1,0:T(8,128)(2,1)S(1)} %pad_maximum_fusion), channel_id=1, source_target_pairs={{0,24},{8,16},{16,8},{24,0},{1,25},{9,17},{17,9},{25,1},{2,26},{10... | collective-permute-start | bytes 202760 | tf_op jit(solution)/shard_map/ppermute | solution.py:62
  9.6 6.0 %collective-permute-start.2 = (bf16[8,4224]{1,0:T(8,128)(2,1)S(1)}, bf16[8,4224]{1,0:T(8,128)(2,1)S(1)}, u32[]{:S(2)}, u32[]{:S(2)}) collective-permute-start(bf16[8,4224]{1,0:T(8,128)(2,1)S(1)} %pad_maximum_fusion), channel_id=1, source_target_pairs={{0,16},{8,24},{16,0},{24,8},{1,17},{9,25},{17,1},{25,9},{2,18},{10... | collective-permute-start | bytes 202760 | tf_op jit(solution)/shard_map/ppermute | solution.py:62
  9.6 6.0 %collective-permute-start.1 = (bf16[8,4224]{1,0:T(8,128)(2,1)S(1)}, bf16[8,4224]{1,0:T(8,128)(2,1)S(1)}, u32[]{:S(2)}, u32[]{:S(2)}) collective-permute-start(bf16[8,4224]{1,0:T(8,128)(2,1)S(1)} %pad_maximum_fusion), channel_id=1, source_target_pairs={{0,8},{8,0},{16,24},{24,16},{1,9},{9,1},{17,25},{25,17},{2,10},{10... | collective-permute-start | bytes 202760 | tf_op jit(solution)/shard_map/ppermute | solution.py:62
  15.7 6.5 %collective-permute-start.4 = (bf16[32,4224]{1,0:T(8,128)(2,1)S(1)}, bf16[32,4224]{1,0:T(8,128)(2,1)S(1)}, u32[]{:S(2)}, u32[]{:S(2)}) collective-permute-start(bf16[32,4224]{1,0:T(8,128)(2,1)S(1)} %concatenate.24), channel_id=1, source_target_pairs={{0,1},{1,0},{2,3},{3,2},{4,6},{5,7},{6,4},{7,5},{8,9},{9,8},{10,11... | collective-permute-start | bytes 811016 | tf_op jit(solution)/shard_map/ppermute | solution.py:63
  22.5 9.4 %collective-permute-start.5 = (bf16[64,4224]{1,0:T(8,128)(2,1)S(1)}, bf16[64,4224]{1,0:T(8,128)(2,1)S(1)}, u32[]{:S(2)}, u32[]{:S(2)}) collective-permute-start(bf16[64,4224]{1,0:T(8,128)(2,1)S(1)} %concatenate.25), channel_id=1, source_target_pairs={{0,2},{1,3},{2,0},{3,1},{4,5},{5,4},{6,7},{7,6},{8,10},{9,11},{10,... | collective-permute-start | bytes 1622024 | tf_op jit(solution)/shard_map/ppermute | solution.py:64
  32.3 2.8 %collective-permute-start.6 = (bf16[128,4224]{1,0:T(8,128)(2,1)S(1)}, bf16[128,4224]{1,0:T(8,128)(2,1)S(1)}, u32[]{:S(2)}, u32[]{:S(2)}) collective-permute-start(bf16[128,4224]{1,0:T(8,128)(2,1)S(1)} %concatenate.26), channel_id=1, source_target_pairs={{0,4},{4,0},{1,5},{5,1},{2,6},{6,2},{3,7},{7,3},{8,12},{12,8},{9,1... | collective-permute-start | bytes 3244040 | tf_op jit(solution)/shard_map/ppermute | solution.py:65
  35.2 5.6 %slice-start.2 = ((s8[6291456]{0:T(1024)(128)(4,1)}), s8[4194304]{0:T(1024)(128)(4,1)S(1)}, s32[]{:S(2)}) async-start(s8[6291456]{0:T(1024)(128)(4,1)} %bitcast.51), calls=%async_computation.2 | async-start | bytes 8388608
  35.4 5.4 %slice-start.3 = ((s8[6291456]{0:T(1024)(128)(4,1)}), s8[2097152]{0:T(1024)(128)(4,1)S(1)}, s32[]{:S(2)}) async-start(s8[6291456]{0:T(1024)(128)(4,1)} %bitcast.51), calls=%async_computation.3 | async-start | bytes 4194304
  48.3 4.1 %slice-start = ((s8[6291456]{0:T(1024)(128)(4,1)}), s8[2097152]{0:T(1024)(128)(4,1)S(1)}, s32[]{:S(2)}) async-start(s8[6291456]{0:T(1024)(128)(4,1)} %bitcast.38), calls=%async_computation | async-start | bytes 4194304
  48.5 4.5 %slice-start.1 = ((s8[6291456]{0:T(1024)(128)(4,1)}), s8[4194304]{0:T(1024)(128)(4,1)S(1)}, s32[]{:S(2)}) async-start(s8[6291456]{0:T(1024)(128)(4,1)} %bitcast.38), calls=%async_computation.1 | async-start | bytes 8388608
  54.2 2.0 %collective-permute-start.7 = (bf16[64,4096]{1,0:T(8,128)(2,1)S(1)}, bf16[64,4096]{1,0:T(8,128)(2,1)S(1)}, u32[]{:S(2)}, u32[]{:S(2)}) collective-permute-start(bf16[64,4096]{1,0:T(8,128)(2,1)S(1)} %select_convert_fusion), channel_id=1, source_target_pairs={{0,4},{4,0},{1,5},{5,1},{2,6},{6,2},{3,7},{7,3},{8,12},{12,8},{9,1... | collective-permute-start | bytes 1572872 | tf_op jit(solution)/shard_map/ppermute | solution.py:97
  56.6 6.4 %collective-permute-start.8 = (bf16[32,4096]{1,0:T(8,128)(2,1)S(1)}, bf16[32,4096]{1,0:T(8,128)(2,1)S(1)}, u32[]{:S(2)}, u32[]{:S(2)}) collective-permute-start(bf16[32,4096]{1,0:T(8,128)(2,1)S(1)} %slice.110), channel_id=1, source_target_pairs={{0,2},{1,3},{2,0},{3,1},{4,5},{5,4},{6,7},{7,6},{8,10},{9,11},{10,... | collective-permute-start | bytes 786440 | tf_op jit(solution)/shard_map/ppermute | solution.py:104
  63.1 5.0 %collective-permute-start.9 = (bf16[16,4096]{1,0:T(8,128)(2,1)S(1)}, bf16[16,4096]{1,0:T(8,128)(2,1)S(1)}, u32[]{:S(2)}, u32[]{:S(2)}) collective-permute-start(bf16[16,4096]{1,0:T(8,128)(2,1)S(1)} %slice.111), channel_id=1, source_target_pairs={{0,1},{1,0},{2,3},{3,2},{4,6},{5,7},{6,4},{7,5},{8,9},{9,8},{10,11... | collective-permute-start | bytes 393224 | tf_op jit(solution)/shard_map/ppermute | solution.py:104
  68.2 4.4 %collective-permute-start.10 = (bf16[4,4096]{1,0:T(4,128)(2,1)S(1)}, bf16[4,4096]{1,0:T(4,128)(2,1)S(1)}, u32[]{:S(2)}, u32[]{:S(2)}) collective-permute-start(bf16[4,4096]{1,0:T(4,128)(2,1)S(1)} %get-tuple-element.7), channel_id=1, source_target_pairs={{0,8},{8,0},{16,24},{24,16},{1,9},{9,1},{17,25},{25,17},{2,10},{10... | collective-permute-start | bytes 98312 | tf_op jit(solution)/shard_map/ppermute | solution.py:104
  69.4 5.7 %collective-permute-start.12 = (bf16[4,4096]{1,0:T(4,128)(2,1)S(1)}, bf16[4,4096]{1,0:T(4,128)(2,1)S(1)}, u32[]{:S(2)}, u32[]{:S(2)}) collective-permute-start(bf16[4,4096]{1,0:T(4,128)(2,1)S(1)} %get-tuple-element.8), channel_id=1, source_target_pairs={{0,24},{8,16},{16,8},{24,0},{1,25},{9,17},{17,9},{25,1},{2,26},{10... | collective-permute-start | bytes 98312 | tf_op jit(solution)/shard_map/ppermute | solution.py:104
  71.0 4.8 %collective-permute-start.11 = (bf16[4,4096]{1,0:T(4,128)(2,1)S(1)}, bf16[4,4096]{1,0:T(4,128)(2,1)S(1)}, u32[]{:S(2)}, u32[]{:S(2)}) collective-permute-start(bf16[4,4096]{1,0:T(4,128)(2,1)S(1)} %get-tuple-element.9), channel_id=1, source_target_pairs={{0,16},{8,24},{16,0},{24,8},{1,17},{9,25},{17,1},{25,9},{2,18},{10... | collective-permute-start | bytes 98312 | tf_op jit(solution)/shard_map/ppermute | solution.py:104
